TPU v7x, 128 devices: a whole 4x4x4 slice. The times are simulated.
128 devices in a mesh: heads: 2 (over z_hi), slab: 64 (over z_lo, y, x, core).
Axes of the slice: x: 4, y: 4, z: 4 (z_hi: 2, z_lo: 2; z = z_hi * 2 + z_lo), core: 2. Of those that a mesh axis runs over, the one named last changes fastest.
Arguments:
- tokens: bfloat16 [64, 384, 3072], P('slab', 'heads'), may hold values from -400 to 400
- qkv_weight: bfloat16 [3072, 4608], P(None, 'heads'), may hold values from -1 to 1
- out_weight: bfloat16 [1536, 3072], P('heads'), may hold values from -0.15625 to 0.15625
- query_gain: float32 [128], replicated, may hold values from 0.6 to 4.5
- key_gain: float32 [128], replicated, may hold values from 0.6 to 4.5
- mod_shift: float32 [3072], replicated, may hold values from -3 to 3
- mod_scale: float32 [3072], replicated, may hold values from -0.5 to 1.5
- branch_gate: float32 [3072], replicated, may hold values from 1 to 3
- block_mask: int32 [64, 27], P('slab'), may hold values 0 or 1
Outputs:
- attended: bfloat16 [64, 384, 3072], P('slab', 'heads')
All inputs are finite; a program needn't handle non-finite values. No bound on the sum of `block_mask` on one device may be relied on, other than what follows from the above.
Results may differ from a plain program's by a relative error of at most 0.0095.
The roundings to bfloat16 on the way count: a program that leaves them out, or rounds other values in their place, can miss the bound.
Values may be sent and summed in bfloat16 or wider, within the bound.
No kernel may reach another device: no remote copies, remote signals or barrier semaphores. Data moves between devices by JAX's collectives and lax.ppermute only.
A program may use at most 320 MiB of HBM per device.

v0:
```python
import jax
import jax.numpy as jnp
from jax import lax
from jax.sharding import PartitionSpec as P

GT = 4


def shifted(value, axis, steps):
    count = lax.axis_size(axis)
    leading, last = (max(0, -steps), min(count, count - steps))
    return lax.ppermute(value, axis, [(source, source + steps) for source in range(leading, last)])


def modulate(token_rows, mod_shift, mod_scale):
    token_rows = token_rows.astype(jnp.float32)
    row_mean = jnp.mean(token_rows, axis=-1, keepdims=True)
    centered = token_rows - row_mean
    variance = jnp.mean(centered * centered, axis=-1, keepdims=True)
    return (centered * lax.rsqrt(variance + 1e-06) * (1.0 + mod_scale) + mod_shift).astype(
        jnp.bfloat16
    )


def head_norm(head_rows, scale_gain):
    head_rows = head_rows.astype(jnp.float32)
    return (
        head_rows
        * lax.rsqrt(jnp.mean(head_rows * head_rows, axis=-1, keepdims=True) + 1e-06)
        * scale_gain
    )


def window_live(mask_row, slab_at, grid_t, grid_h, grid_w):
    time_at = slab_at // (grid_h * grid_w)
    height_at = slab_at // grid_w % grid_h
    width_at = slab_at % grid_w
    offsets = jnp.arange(27, dtype=jnp.int32)
    step_t = offsets // 9 - 1
    step_h = offsets // 3 % 3 - 1
    step_w = offsets % 3 - 1
    inside = (time_at + step_t >= 0) & (time_at + step_t < grid_t)
    inside = inside & (height_at + step_h >= 0) & (height_at + step_h < grid_h)
    inside = inside & (width_at + step_w >= 0) & (width_at + step_w < grid_w)
    return inside & ((offsets == 13) | (mask_row == 1))


def soft_weights(scores, live):
    keep = live[None, :, None]
    masked = jnp.where(keep, scores, -1e30)
    row_top = jnp.max(masked, axis=(1, 2), keepdims=True)
    raised = jnp.where(keep, jnp.exp(masked - row_top), 0.0)
    return (raised / jnp.sum(raised, axis=(1, 2), keepdims=True)).astype(jnp.bfloat16)


def collect_window(packed, grid_h, grid_w):
    plane = grid_h * grid_w
    blocks = []
    for order_at in range(27):
        if order_at == 13:
            blocks.append(packed)
        else:
            offset = (
                (order_at // 9 - 1) * plane + (order_at // 3 % 3 - 1) * grid_w + (order_at % 3 - 1)
            )
            blocks.append(shifted(packed, "slab", -offset))
    return jnp.concatenate(blocks, axis=0)


def on_device(
    tokens,
    qkv_weight,
    out_weight,
    query_gain,
    key_gain,
    mod_shift,
    mod_scale,
    branch_gate,
    block_mask,
):
    head_dim = query_gain.shape[0]
    group_width = out_weight.shape[0]
    group_heads = group_width // head_dim
    normed = modulate(tokens[0], mod_shift, mod_scale)
    projected = jnp.dot(
        lax.all_gather(normed, "heads", axis=0, tiled=True),
        qkv_weight,
        preferred_element_type=jnp.float32,
    ).astype(jnp.bfloat16)
    tile_tok = projected.shape[0]
    pieces = projected.reshape(tile_tok, group_heads, 3, head_dim)
    queries = (head_norm(pieces[:, :, 0], query_gain) * head_dim ** (-0.5)).astype(jnp.bfloat16)
    own_keys = head_norm(pieces[:, :, 1], key_gain).astype(jnp.bfloat16)
    packed = jnp.concatenate(
        [own_keys.reshape(tile_tok, group_width), pieces[:, :, 2].reshape(tile_tok, group_width)],
        axis=1,
    )[None]
    slab_count = lax.axis_size("slab")
    slab_at = lax.axis_index("slab")
    grid_h = min(4, slab_count // 8)
    grid_w = slab_count // (GT * grid_h)
    window = collect_window(packed, grid_h, grid_w)
    window_keys = window[:, :, :group_width].reshape(27, tile_tok, group_heads, head_dim)
    window_values = window[:, :, group_width:].reshape(27, tile_tok, group_heads, head_dim)
    live = window_live(block_mask[0], slab_at, GT, grid_h, grid_w)

    def one_head(head_at):
        query_rows = lax.dynamic_index_in_dim(queries, head_at, 1, keepdims=False)
        key_rows = lax.dynamic_index_in_dim(window_keys, head_at, 2, keepdims=False)
        value_rows = lax.dynamic_index_in_dim(window_values, head_at, 2, keepdims=False)
        scores = jnp.einsum("qd,okd->qok", query_rows, key_rows, preferred_element_type=jnp.float32)
        weights = soft_weights(scores, live)
        return jnp.einsum(
            "qok,okd->qd", weights, value_rows, preferred_element_type=jnp.float32
        ).astype(jnp.bfloat16)

    per_head = lax.map(one_head, jnp.arange(group_heads, dtype=jnp.int32))
    attention = jnp.transpose(per_head, (1, 0, 2)).reshape(tile_tok, group_width)
    summed = lax.psum_scatter(
        jnp.dot(attention, out_weight, preferred_element_type=jnp.float32).astype(jnp.bfloat16),
        "heads",
        scatter_dimension=0,
        tiled=True,
    ).astype(jnp.float32)
    return (branch_gate * summed).astype(jnp.bfloat16)[None]


def solution(mesh):
    in_specs = (
        P("slab", "heads", None),
        P(None, "heads"),
        P("heads", None),
        P(),
        P(),
        P(),
        P(),
        P(),
        P("slab", None),
    )
    out_specs = P("slab", "heads", None)
    return jax.shard_map(
        on_device, mesh=mesh, in_specs=in_specs, out_specs=out_specs, check_vma=False
    )
```

profile of v0, /device:TPU:1, one launch (start us, length us, event | category | flops | bytes accessed | tf_op | source)
XLA Modules:
  0.0 1011.1 jit_solution(6357708120327719233)
XLA Ops:
  7.3 1.5 convert_reduce_fusion
  8.8 1.7 fusion.25
  10.5 2.8 fusion.28
  13.4 43.4 %all-gather.2.cloned.1.call-done = bf16[384,3072]{1,0:T(8,128)(2,1)} async-done(((bf16[192,3072]{1,0:T(8,128)(2,1)}), bf16[384,3072]{1,0:T(8,128)(2,1)}) %all-gather.2.cloned.1.call-update) | async-done | bytes 2359312 | tf_op jit(solution)/shard_map/all_gather | solution.py:86
  56.8 11.2 %convolution_convert_fusion.1 = bf16[384,2304]{1,0:T(8,128)(2,1)S(1)} fusion(bf16[384,3072]{1,0:T(8,128)(2,1)} %all-gather.2.cloned.1.call-done, bf16[3072,2304]{1,0:T(8,128)(2,1)} %param.12), kind=kOutput, calls=%fused_computation.21 | convolution fusion | flops 5436702720 | bytes 18284544 | tf_op jit(solution)/shard_map/dot_general | solution.py:85
  70.8 8.5 collective-permute-start
  79.3 2.5 collective-permute-start.1
  81.9 6.1 collective-permute-start.2
  88.0 1.4 collective-permute-start.3
  89.4 1.4 collective-permute-start.4
  91.1 7.6 collective-permute-done
  98.7 24.0 %collective-permute-start.5 = (bf16[1,384,1536]{1,2,0:T(8,128)(2,1)}, bf16[1,384,1536]{1,2,0:T(8,128)(2,1)S(1)}, u32[]{:S(2)}, u32[]{:S(2)}) collective-permute-start(bf16[1,384,1536]{1,2,0:T(8,128)(2,1)} %maximum_bitcast_fusion), channel_id=1, source_target_pairs={{0,15},{1,16},{2,17},{3,18},{4,19},{5,20},{6,21},{7,22},{8,23},{9,... | collective-permute-start | bytes 3538952 | tf_op jit(solution)/shard_map/ppermute | solution.py:12
  122.7 1.4 constant_dynamic-update-slice_fusion.27
  124.2 47.3 %collective-permute-start.6 = (bf16[1,384,1536]{1,2,0:T(8,128)(2,1)}, bf16[1,384,1536]{1,2,0:T(8,128)(2,1)S(1)}, u32[]{:S(2)}, u32[]{:S(2)}) collective-permute-start(bf16[1,384,1536]{1,2,0:T(8,128)(2,1)} %maximum_bitcast_fusion), channel_id=1, source_target_pairs={{0,13},{1,14},{2,15},{3,16},{4,17},{5,18},{6,19},{7,20},{8,21},{9,... | collective-permute-start | bytes 3538952 | tf_op jit(solution)/shard_map/ppermute | solution.py:12
  171.5 1.5 constant_dynamic-update-slice_fusion.26
  173.0 21.9 %collective-permute-start.7 = (bf16[1,384,1536]{1,2,0:T(8,128)(2,1)}, bf16[1,384,1536]{1,2,0:T(8,128)(2,1)S(1)}, u32[]{:S(2)}, u32[]{:S(2)}) collective-permute-start(bf16[1,384,1536]{1,2,0:T(8,128)(2,1)} %maximum_bitcast_fusion), channel_id=1, source_target_pairs={{0,12},{1,13},{2,14},{3,15},{4,16},{5,17},{6,18},{7,19},{8,20},{9,... | collective-permute-start | bytes 3538952 | tf_op jit(solution)/shard_map/ppermute | solution.py:12
  194.9 1.5 constant_dynamic-update-slice_fusion.25
  196.4 39.4 %collective-permute-start.8 = (bf16[1,384,1536]{1,2,0:T(8,128)(2,1)}, bf16[1,384,1536]{1,2,0:T(8,128)(2,1)S(1)}, u32[]{:S(2)}, u32[]{:S(2)}) collective-permute-start(bf16[1,384,1536]{1,2,0:T(8,128)(2,1)} %maximum_bitcast_fusion), channel_id=1, source_target_pairs={{0,11},{1,12},{2,13},{3,14},{4,15},{5,16},{6,17},{7,18},{8,19},{9,... | collective-permute-start | bytes 3538952 | tf_op jit(solution)/shard_map/ppermute | solution.py:12
  236.1 100.3 %collective-permute-start.9 = (bf16[1,384,1536]{1,2,0:T(8,128)(2,1)}, bf16[1,384,1536]{1,2,0:T(8,128)(2,1)S(1)}, u32[]{:S(2)}, u32[]{:S(2)}) collective-permute-start(bf16[1,384,1536]{1,2,0:T(8,128)(2,1)} %maximum_bitcast_fusion), channel_id=1, source_target_pairs={{0,5},{1,6},{2,7},{3,8},{4,9},{5,10},{6,11},{7,12},{8,13},{9,14},{... | collective-permute-start | bytes 3538952 | tf_op jit(solution)/shard_map/ppermute | solution.py:12
  336.7 1.4 collective-permute-start.10
  338.3 1.4 collective-permute-start.11
  340.0 3.3 collective-permute-start.12
  343.6 1.9 collective-permute-start.13
  345.7 31.7 %collective-permute-done.9 = bf16[1,384,1536]{1,2,0:T(8,128)(2,1)S(1)} collective-permute-done((bf16[1,384,1536]{1,2,0:T(8,128)(2,1)}, bf16[1,384,1536]{1,2,0:T(8,128)(2,1)S(1)}, u32[]{:S(2)}, u32[]{:S(2)}) %collective-permute-start.9) | collective-permute-done | bytes 1179680 | tf_op jit(solution)/shard_map/ppermute | solution.py:12
  378.9 1.3 collective-permute-start.15
  380.5 2.9 collective-permute-done.11
  385.0 11.1 %collective-permute-done.12 = bf16[1,384,1536]{1,2,0:T(8,128)(2,1)S(1)} collective-permute-done((bf16[1,384,1536]{1,2,0:T(8,128)(2,1)}, bf16[1,384,1536]{1,2,0:T(8,128)(2,1)S(1)}, u32[]{:S(2)}, u32[]{:S(2)}) %collective-permute-start.12) | collective-permute-done | bytes 1179680 | tf_op jit(solution)/shard_map/ppermute | solution.py:12
  397.8 2.6 collective-permute-done.13
  401.9 39.6 %collective-permute-done.14 = bf16[1,384,1536]{1,2,0:T(8,128)(2,1)S(1)} collective-permute-done((bf16[1,384,1536]{1,2,0:T(8,128)(2,1)}, bf16[1,384,1536]{1,2,0:T(8,128)(2,1)S(1)}, u32[]{:S(2)}, u32[]{:S(2)}) %collective-permute-start.14) | collective-permute-done | bytes 1179680 | tf_op jit(solution)/shard_map/ppermute | solution.py:12
  441.5 1.3 collective-permute-start.19
  443.1 1.5 collective-permute-start.20
  444.8 34.9 %collective-permute-done.16 = bf16[1,384,1536]{1,2,0:T(8,128)(2,1)S(1)} collective-permute-done((bf16[1,384,1536]{1,2,0:T(8,128)(2,1)}, bf16[1,384,1536]{1,2,0:T(8,128)(2,1)S(1)}, u32[]{:S(2)}, u32[]{:S(2)}) %collective-permute-start.16) | collective-permute-done | bytes 1179680 | tf_op jit(solution)/shard_map/ppermute | solution.py:12
  479.6 1.3 collective-permute-start.21
  481.2 7.9 collective-permute-done.17
  489.1 1.3 collective-permute-start.22
  490.6 13.7 %collective-permute-done.18 = bf16[1,384,1536]{1,2,0:T(8,128)(2,1)S(1)} collective-permute-done((bf16[1,384,1536]{1,2,0:T(8,128)(2,1)}, bf16[1,384,1536]{1,2,0:T(8,128)(2,1)S(1)}, u32[]{:S(2)}, u32[]{:S(2)}) %collective-permute-start.18) | collective-permute-done | bytes 1179680 | tf_op jit(solution)/shard_map/ppermute | solution.py:12
  505.8 43.6 %collective-permute-done.19 = bf16[1,384,1536]{1,2,0:T(8,128)(2,1)S(1)} collective-permute-done((bf16[1,384,1536]{1,2,0:T(8,128)(2,1)}, bf16[1,384,1536]{1,2,0:T(8,128)(2,1)S(1)}, u32[]{:S(2)}, u32[]{:S(2)}) %collective-permute-start.19) | collective-permute-done | bytes 1179680 | tf_op jit(solution)/shard_map/ppermute | solution.py:12
  551.0 1.3 collective-permute-start.25
  552.8 4.7 collective-permute-done.22
  557.8 91.0 %collective-permute-done.23 = bf16[1,384,1536]{1,2,0:T(8,128)(2,1)S(1)} collective-permute-done((bf16[1,384,1536]{1,2,0:T(8,128)(2,1)}, bf16[1,384,1536]{1,2,0:T(8,128)(2,1)S(1)}, u32[]{:S(2)}, u32[]{:S(2)}) %collective-permute-start.23) | collective-permute-done | bytes 1179680 | tf_op jit(solution)/shard_map/ppermute | solution.py:12
  649.3 55.4 %collective-permute-done.25 = bf16[1,384,1536]{1,2,0:T(8,128)(2,1)S(1)} collective-permute-done((bf16[1,384,1536]{1,2,0:T(8,128)(2,1)}, bf16[1,384,1536]{1,2,0:T(8,128)(2,1)S(1)}, u32[]{:S(2)}, u32[]{:S(2)}) %collective-permute-start.25) | collective-permute-done | bytes 1179680 | tf_op jit(solution)/shard_map/ppermute | solution.py:12
  704.9 10.8 %fusion.44 = (bf16[27,384,768]{1,2,0:T(8,128)(2,1)}, bf16[27,384,768]{1,2,0:T(8,128)(2,1)}) fusion(bf16[27,384,1536]{1,2,0:T(8,128)(2,1)S(1)} %constant_dynamic-update-slice_fusion.1), kind=kLoop, calls=%fused_computation.97 | loop fusion | bytes 63700992 | tf_op jit(solution)/shard_map/slice | solution.py:104
  715.8 193.5 %while.10 = (s32[]{:T(128)}, bf16[6,384,128]{1,2,0:T(8,128)(2,1)S(1)}, pred[27]{0:T(512)(128)(4,1)S(1)}, s32[6]{0:T(128)S(1)}, bf16[384,6,128]{0,2,1:T(8,128)(2,...) while((s32[]{:T(128)}, ...), condition=%wide.region_7.8_spmd, body=%wide.region_4.7_spmd.sunk | while | flops 2082274560 | bytes 53683416 | solution.py:117
  718.3 9.9 select_reduce_fusion.2
  728.2 9.3 fusion.53
  737.5 10.4 %fusion.54 = bf16[1,384,128]{2,1,0:T(8,128)(2,1)S(1)} fusion(bf16[27,384,6,128]{1,3,2,0:T(8,128)(2,1)} %get-tuple-element.143, s32[]{:T(128)S(6)} %select_n.126, f32[384,27,384]{0,2,1:T(8,128)} %get-tuple-element.115, f32[384]{0:T(512)S(1)} %fusion.53, f32[384]{0:T(512)S(1)} %get-tuple-element.116, pred[27]{0:T(512)(128)(4,1)S(1)} %get-tuple-element.139), kind=kOutput, calls=%fused_computation.12.clone.1 | convolution fusion | flops 1039171584 | bytes 18680864 | tf_op jit(solution)/shard_map/while/body/eval_jaxpr/qok,okd->qd/dot_general | solution.py:113
  750.6 9.9 select_reduce_fusion.2
  760.5 9.3 fusion.53
  769.7 10.4 %fusion.54 = bf16[1,384,128]{2,1,0:T(8,128)(2,1)S(1)} fusion(bf16[27,384,6,128]{1,3,2,0:T(8,128)(2,1)} %get-tuple-element.143, s32[]{:T(128)S(6)} %select_n.126, f32[384,27,384]{0,2,1:T(8,128)} %get-tuple-element.115, f32[384]{0:T(512)S(1)} %fusion.53, f32[384]{0:T(512)S(1)} %get-tuple-element.116, pred[27]{0:T(512)(128)(4,1)S(1)} %get-tuple-element.139), kind=kOutput, calls=%fused_computation.12.clone.1 | convolution fusion | flops 1039171584 | bytes 18680864 | tf_op jit(solution)/shard_map/while/body/eval_jaxpr/qok,okd->qd/dot_general | solution.py:113
  782.8 9.9 select_reduce_fusion.2
  792.7 9.3 fusion.53
  802.0 10.4 %fusion.54 = bf16[1,384,128]{2,1,0:T(8,128)(2,1)S(1)} fusion(bf16[27,384,6,128]{1,3,2,0:T(8,128)(2,1)} %get-tuple-element.143, s32[]{:T(128)S(6)} %select_n.126, f32[384,27,384]{0,2,1:T(8,128)} %get-tuple-element.115, f32[384]{0:T(512)S(1)} %fusion.53, f32[384]{0:T(512)S(1)} %get-tuple-element.116, pred[27]{0:T(512)(128)(4,1)S(1)} %get-tuple-element.139), kind=kOutput, calls=%fused_computation.12.clone.1 | convolution fusion | flops 1039171584 | bytes 18680864 | tf_op jit(solution)/shard_map/while/body/eval_jaxpr/qok,okd->qd/dot_general | solution.py:113
  815.1 9.9 select_reduce_fusion.2
  825.0 9.3 fusion.53
  834.2 10.4 %fusion.54 = bf16[1,384,128]{2,1,0:T(8,128)(2,1)S(1)} fusion(bf16[27,384,6,128]{1,3,2,0:T(8,128)(2,1)} %get-tuple-element.143, s32[]{:T(128)S(6)} %select_n.126, f32[384,27,384]{0,2,1:T(8,128)} %get-tuple-element.115, f32[384]{0:T(512)S(1)} %fusion.53, f32[384]{0:T(512)S(1)} %get-tuple-element.116, pred[27]{0:T(512)(128)(4,1)S(1)} %get-tuple-element.139), kind=kOutput, calls=%fused_computation.12.clone.1 | convolution fusion | flops 1039171584 | bytes 18680864 | tf_op jit(solution)/shard_map/while/body/eval_jaxpr/qok,okd->qd/dot_general | solution.py:113
  847.3 9.9 select_reduce_fusion.2
  857.2 9.3 fusion.53
  866.5 10.4 %fusion.54 = bf16[1,384,128]{2,1,0:T(8,128)(2,1)S(1)} fusion(bf16[27,384,6,128]{1,3,2,0:T(8,128)(2,1)} %get-tuple-element.143, s32[]{:T(128)S(6)} %select_n.126, f32[384,27,384]{0,2,1:T(8,128)} %get-tuple-element.115, f32[384]{0:T(512)S(1)} %fusion.53, f32[384]{0:T(512)S(1)} %get-tuple-element.116, pred[27]{0:T(512)(128)(4,1)S(1)} %get-tuple-element.139), kind=kOutput, calls=%fused_computation.12.clone.1 | convolution fusion | flops 1039171584 | bytes 18680864 | tf_op jit(solution)/shard_map/while/body/eval_jaxpr/qok,okd->qd/dot_general | solution.py:113
  879.6 9.9 select_reduce_fusion.2
  889.5 9.3 fusion.53
  898.8 10.4 %fusion.54 = bf16[1,384,128]{2,1,0:T(8,128)(2,1)S(1)} fusion(bf16[27,384,6,128]{1,3,2,0:T(8,128)(2,1)} %get-tuple-element.143, s32[]{:T(128)S(6)} %select_n.126, f32[384,27,384]{0,2,1:T(8,128)} %get-tuple-element.115, f32[384]{0:T(512)S(1)} %fusion.53, f32[384]{0:T(512)S(1)} %get-tuple-element.116, pred[27]{0:T(512)(128)(4,1)S(1)} %get-tuple-element.139), kind=kOutput, calls=%fused_computation.12.clone.1 | convolution fusion | flops 1039171584 | bytes 18680864 | tf_op jit(solution)/shard_map/while/body/eval_jaxpr/qok,okd->qd/dot_general | solution.py:113
  909.3 5.8 convolution_convert_fusion
  915.2 86.5 %reduce-scatter.2.cloned.1.call-done = bf16[192,3072]{1,0:T(8,128)(2,1)} async-done(((bf16[384,3072]{1,0:T(8,128)(2,1)}), bf16[192,3072]{1,0:T(8,128)(2,1)}) %reduce-scatter.2.cloned.1.call-update) | async-done | bytes 1179664 | tf_op jit(solution)/shard_map/reduce_scatter | solution.py:119
  1001.7 2.5 fusion.33
  (93 shorter events, 21.7 us)
Async XLA Ops:
  6.5 6.9 copy-start
  6.5 50.3 %all-gather.2.cloned.1.call-start = ((), (), s32[]{:S(2)}) async-start(), calls=%async_computation.1 | async-start | bytes 3538944 | tf_op jit(solution)/shard_map/all_gather | solution.py:86
  13.4 988.3 %reduce-scatter.2.cloned.1.call-start = ((), (), s32[]{:S(2)}) async-start(), calls=%async_computation.2 | async-start | bytes 3538944 | tf_op jit(solution)/shard_map/reduce_scatter | solution.py:119
  69.2 18.8 %copy-start.5 = (s32[1,27]{1,0:T(1,128)S(1)}, s32[1,27]{1,0:T(1,128)}, u32[]{:S(2)}) copy-start(s32[1,27]{1,0:T(1,128)} %param.19) | copy-start | bytes 328
  69.2 21.8 %copy-start.4 = (f32[128]{0:T(128)S(1)}, f32[128]{0:T(128)}, u32[]{:S(2)}) copy-start(f32[128]{0:T(128)} %param.14) | copy-start | bytes 1540
  70.8 27.9 %collective-permute-start = (bf16[1,384,1536]{1,2,0:T(8,128)(2,1)}, bf16[1,384,1536]{1,2,0:T(8,128)(2,1)}, u32[]{:S(2)}, u32[]{:S(2)}) collective-permute-start(bf16[1,384,1536]{1,2,0:T(8,128)(2,1)} %maximum_bitcast_fusion), channel_id=1, source_target_pairs={{0,21},{1,22},{2,23},{3,24},{4,25},{5,26},{6,27},{7,28},{8,29},{9,... | collective-permute-start | bytes 3538952 | tf_op jit(solution)/shard_map/ppermute | solution.py:12
  79.3 44.8 %collective-permute-start.1 = (bf16[1,384,1536]{1,2,0:T(8,128)(2,1)}, bf16[1,384,1536]{1,2,0:T(8,128)(2,1)}, u32[]{:S(2)}, u32[]{:S(2)}) collective-permute-start(bf16[1,384,1536]{1,2,0:T(8,128)(2,1)} %maximum_bitcast_fusion), channel_id=1, source_target_pairs={{0,20},{1,21},{2,22},{3,23},{4,24},{5,25},{6,26},{7,27},{8,28},{9,... | collective-permute-start | bytes 3538952 | tf_op jit(solution)/shard_map/ppermute | solution.py:12
  81.9 91.1 %collective-permute-start.2 = (bf16[1,384,1536]{1,2,0:T(8,128)(2,1)}, bf16[1,384,1536]{1,2,0:T(8,128)(2,1)}, u32[]{:S(2)}, u32[]{:S(2)}) collective-permute-start(bf16[1,384,1536]{1,2,0:T(8,128)(2,1)} %maximum_bitcast_fusion), channel_id=1, source_target_pairs={{0,19},{1,20},{2,21},{3,22},{4,23},{5,24},{6,25},{7,26},{8,27},{9,... | collective-permute-start | bytes 3538952 | tf_op jit(solution)/shard_map/ppermute | solution.py:12
  88.0 108.4 %collective-permute-start.3 = (bf16[1,384,1536]{1,2,0:T(8,128)(2,1)}, bf16[1,384,1536]{1,2,0:T(8,128)(2,1)S(1)}, u32[]{:S(2)}, u32[]{:S(2)}) collective-permute-start(bf16[1,384,1536]{1,2,0:T(8,128)(2,1)} %maximum_bitcast_fusion), channel_id=1, source_target_pairs={{0,17},{1,18},{2,19},{3,20},{4,21},{5,22},{6,23},{7,24},{8,25},{9,... | collective-permute-start | bytes 3538952 | tf_op jit(solution)/shard_map/ppermute | solution.py:12
  89.4 146.7 %collective-permute-start.4 = (bf16[1,384,1536]{1,2,0:T(8,128)(2,1)}, bf16[1,384,1536]{1,2,0:T(8,128)(2,1)S(1)}, u32[]{:S(2)}, u32[]{:S(2)}) collective-permute-start(bf16[1,384,1536]{1,2,0:T(8,128)(2,1)} %maximum_bitcast_fusion), channel_id=1, source_target_pairs={{0,16},{1,17},{2,18},{3,19},{4,20},{5,21},{6,22},{7,23},{8,24},{9,... | collective-permute-start | bytes 3538952 | tf_op jit(solution)/shard_map/ppermute | solution.py:12
  98.7 238.0 %collective-permute-start.5 = (bf16[1,384,1536]{1,2,0:T(8,128)(2,1)}, bf16[1,384,1536]{1,2,0:T(8,128)(2,1)S(1)}, u32[]{:S(2)}, u32[]{:S(2)}) collective-permute-start(bf16[1,384,1536]{1,2,0:T(8,128)(2,1)} %maximum_bitcast_fusion), channel_id=1, source_target_pairs={{0,15},{1,16},{2,17},{3,18},{4,19},{5,20},{6,21},{7,22},{8,23},{9,... | collective-permute-start | bytes 3538952 | tf_op jit(solution)/shard_map/ppermute | solution.py:12
  124.2 214.2 %collective-permute-start.6 = (bf16[1,384,1536]{1,2,0:T(8,128)(2,1)}, bf16[1,384,1536]{1,2,0:T(8,128)(2,1)S(1)}, u32[]{:S(2)}, u32[]{:S(2)}) collective-permute-start(bf16[1,384,1536]{1,2,0:T(8,128)(2,1)} %maximum_bitcast_fusion), channel_id=1, source_target_pairs={{0,13},{1,14},{2,15},{3,16},{4,17},{5,18},{6,19},{7,20},{8,21},{9,... | collective-permute-start | bytes 3538952 | tf_op jit(solution)/shard_map/ppermute | solution.py:12
  173.0 167.0 %collective-permute-start.7 = (bf16[1,384,1536]{1,2,0:T(8,128)(2,1)}, bf16[1,384,1536]{1,2,0:T(8,128)(2,1)S(1)}, u32[]{:S(2)}, u32[]{:S(2)}) collective-permute-start(bf16[1,384,1536]{1,2,0:T(8,128)(2,1)} %maximum_bitcast_fusion), channel_id=1, source_target_pairs={{0,12},{1,13},{2,14},{3,15},{4,16},{5,17},{6,18},{7,19},{8,20},{9,... | collective-permute-start | bytes 3538952 | tf_op jit(solution)/shard_map/ppermute | solution.py:12
  196.4 147.1 %collective-permute-start.8 = (bf16[1,384,1536]{1,2,0:T(8,128)(2,1)}, bf16[1,384,1536]{1,2,0:T(8,128)(2,1)S(1)}, u32[]{:S(2)}, u32[]{:S(2)}) collective-permute-start(bf16[1,384,1536]{1,2,0:T(8,128)(2,1)} %maximum_bitcast_fusion), channel_id=1, source_target_pairs={{0,11},{1,12},{2,13},{3,14},{4,15},{5,16},{6,17},{7,18},{8,19},{9,... | collective-permute-start | bytes 3538952 | tf_op jit(solution)/shard_map/ppermute | solution.py:12
  236.1 141.3 %collective-permute-start.9 = (bf16[1,384,1536]{1,2,0:T(8,128)(2,1)}, bf16[1,384,1536]{1,2,0:T(8,128)(2,1)S(1)}, u32[]{:S(2)}, u32[]{:S(2)}) collective-permute-start(bf16[1,384,1536]{1,2,0:T(8,128)(2,1)} %maximum_bitcast_fusion), channel_id=1, source_target_pairs={{0,5},{1,6},{2,7},{3,8},{4,9},{5,10},{6,11},{7,12},{8,13},{9,14},{... | collective-permute-start | bytes 3538952 | tf_op jit(solution)/shard_map/ppermute | solution.py:12
  336.7 42.2 %collective-permute-start.10 = (bf16[1,384,1536]{1,2,0:T(8,128)(2,1)}, bf16[1,384,1536]{1,2,0:T(8,128)(2,1)S(1)}, u32[]{:S(2)}, u32[]{:S(2)}) collective-permute-start(bf16[1,384,1536]{1,2,0:T(8,128)(2,1)} %maximum_bitcast_fusion), channel_id=1, source_target_pairs={{0,4},{1,5},{2,6},{3,7},{4,8},{5,9},{6,10},{7,11},{8,12},{9,13},{1... | collective-permute-start | bytes 3538952 | tf_op jit(solution)/shard_map/ppermute | solution.py:12
  338.3 45.1 %collective-permute-start.11 = (bf16[1,384,1536]{1,2,0:T(8,128)(2,1)}, bf16[1,384,1536]{1,2,0:T(8,128)(2,1)S(1)}, u32[]{:S(2)}, u32[]{:S(2)}) collective-permute-start(bf16[1,384,1536]{1,2,0:T(8,128)(2,1)} %maximum_bitcast_fusion), channel_id=1, source_target_pairs={{0,3},{1,4},{2,5},{3,6},{4,7},{5,8},{6,9},{7,10},{8,11},{9,12},{10... | collective-permute-start | bytes 3538952 | tf_op jit(solution)/shard_map/ppermute | solution.py:12
  340.0 56.1 %collective-permute-start.12 = (bf16[1,384,1536]{1,2,0:T(8,128)(2,1)}, bf16[1,384,1536]{1,2,0:T(8,128)(2,1)S(1)}, u32[]{:S(2)}, u32[]{:S(2)}) collective-permute-start(bf16[1,384,1536]{1,2,0:T(8,128)(2,1)} %maximum_bitcast_fusion), channel_id=1, source_target_pairs={{0,1},{1,2},{2,3},{3,4},{4,5},{5,6},{6,7},{7,8},{8,9},{9,10},{10,1... | collective-permute-start | bytes 3538952 | tf_op jit(solution)/shard_map/ppermute | solution.py:12
  343.6 56.8 %collective-permute-start.13 = (bf16[1,384,1536]{1,2,0:T(8,128)(2,1)}, bf16[1,384,1536]{1,2,0:T(8,128)(2,1)S(1)}, u32[]{:S(2)}, u32[]{:S(2)}) collective-permute-start(bf16[1,384,1536]{1,2,0:T(8,128)(2,1)} %maximum_bitcast_fusion), channel_id=1, source_target_pairs={{1,0},{2,1},{3,2},{4,3},{5,4},{6,5},{7,6},{8,7},{9,8},{10,9},{11,1... | collective-permute-start | bytes 3538952 | tf_op jit(solution)/shard_map/ppermute | solution.py:12
  377.4 64.1 %collective-permute-start.14 = (bf16[1,384,1536]{1,2,0:T(8,128)(2,1)}, bf16[1,384,1536]{1,2,0:T(8,128)(2,1)S(1)}, u32[]{:S(2)}, u32[]{:S(2)}) collective-permute-start(bf16[1,384,1536]{1,2,0:T(8,128)(2,1)} %maximum_bitcast_fusion), channel_id=1, source_target_pairs={{3,0},{4,1},{5,2},{6,3},{7,4},{8,5},{9,6},{10,7},{11,8},{12,9},{13... | collective-permute-start | bytes 3538952 | tf_op jit(solution)/shard_map/ppermute | solution.py:12
  378.9 64.1 %collective-permute-start.15 = (bf16[1,384,1536]{1,2,0:T(8,128)(2,1)}, bf16[1,384,1536]{1,2,0:T(8,128)(2,1)S(1)}, u32[]{:S(2)}, u32[]{:S(2)}) collective-permute-start(bf16[1,384,1536]{1,2,0:T(8,128)(2,1)} %maximum_bitcast_fusion), channel_id=1, source_target_pairs={{4,0},{5,1},{6,2},{7,3},{8,4},{9,5},{10,6},{11,7},{12,8},{13,9},{1... | collective-permute-start | bytes 3538952 | tf_op jit(solution)/shard_map/ppermute | solution.py:12
  383.4 96.2 %collective-permute-start.16 = (bf16[1,384,1536]{1,2,0:T(8,128)(2,1)}, bf16[1,384,1536]{1,2,0:T(8,128)(2,1)S(1)}, u32[]{:S(2)}, u32[]{:S(2)}) collective-permute-start(bf16[1,384,1536]{1,2,0:T(8,128)(2,1)} %maximum_bitcast_fusion), channel_id=1, source_target_pairs={{5,0},{6,1},{7,2},{8,3},{9,4},{10,5},{11,6},{12,7},{13,8},{14,9},{... | collective-permute-start | bytes 3538952 | tf_op jit(solution)/shard_map/ppermute | solution.py:12
  396.1 93.0 %collective-permute-start.17 = (bf16[1,384,1536]{1,2,0:T(8,128)(2,1)}, bf16[1,384,1536]{1,2,0:T(8,128)(2,1)S(1)}, u32[]{:S(2)}, u32[]{:S(2)}) collective-permute-start(bf16[1,384,1536]{1,2,0:T(8,128)(2,1)} %maximum_bitcast_fusion), channel_id=1, source_target_pairs={{11,0},{12,1},{13,2},{14,3},{15,4},{16,5},{17,6},{18,7},{19,8},{20... | collective-permute-start | bytes 3538952 | tf_op jit(solution)/shard_map/ppermute | solution.py:12
  400.4 103.9 %collective-permute-start.18 = (bf16[1,384,1536]{1,2,0:T(8,128)(2,1)}, bf16[1,384,1536]{1,2,0:T(8,128)(2,1)S(1)}, u32[]{:S(2)}, u32[]{:S(2)}) collective-permute-start(bf16[1,384,1536]{1,2,0:T(8,128)(2,1)} %maximum_bitcast_fusion), channel_id=1, source_target_pairs={{12,0},{13,1},{14,2},{15,3},{16,4},{17,5},{18,6},{19,7},{20,8},{21... | collective-permute-start | bytes 3538952 | tf_op jit(solution)/shard_map/ppermute | solution.py:12
  441.5 108.0 %collective-permute-start.19 = (bf16[1,384,1536]{1,2,0:T(8,128)(2,1)}, bf16[1,384,1536]{1,2,0:T(8,128)(2,1)S(1)}, u32[]{:S(2)}, u32[]{:S(2)}) collective-permute-start(bf16[1,384,1536]{1,2,0:T(8,128)(2,1)} %maximum_bitcast_fusion), channel_id=1, source_target_pairs={{13,0},{14,1},{15,2},{16,3},{17,4},{18,5},{19,6},{20,7},{21,8},{22... | collective-permute-start | bytes 3538952 | tf_op jit(solution)/shard_map/ppermute | solution.py:12
  443.1 107.9 %collective-permute-start.20 = (bf16[1,384,1536]{1,2,0:T(8,128)(2,1)}, bf16[1,384,1536]{1,2,0:T(8,128)(2,1)S(1)}, u32[]{:S(2)}, u32[]{:S(2)}) collective-permute-start(bf16[1,384,1536]{1,2,0:T(8,128)(2,1)} %maximum_bitcast_fusion), channel_id=1, source_target_pairs={{15,0},{16,1},{17,2},{18,3},{19,4},{20,5},{21,6},{22,7},{23,8},{24... | collective-permute-start | bytes 3538952 | tf_op jit(solution)/shard_map/ppermute | solution.py:12
  479.6 72.9 %collective-permute-start.21 = (bf16[1,384,1536]{1,2,0:T(8,128)(2,1)}, bf16[1,384,1536]{1,2,0:T(8,128)(2,1)S(1)}, u32[]{:S(2)}, u32[]{:S(2)}) collective-permute-start(bf16[1,384,1536]{1,2,0:T(8,128)(2,1)} %maximum_bitcast_fusion), channel_id=1, source_target_pairs={{16,0},{17,1},{18,2},{19,3},{20,4},{21,5},{22,6},{23,7},{24,8},{25... | collective-permute-start | bytes 3538952 | tf_op jit(solution)/shard_map/ppermute | solution.py:12
  489.1 68.5 %collective-permute-start.22 = (bf16[1,384,1536]{1,2,0:T(8,128)(2,1)}, bf16[1,384,1536]{1,2,0:T(8,128)(2,1)S(1)}, u32[]{:S(2)}, u32[]{:S(2)}) collective-permute-start(bf16[1,384,1536]{1,2,0:T(8,128)(2,1)} %maximum_bitcast_fusion), channel_id=1, source_target_pairs={{17,0},{18,1},{19,2},{20,3},{21,4},{22,5},{23,6},{24,7},{25,8},{26... | collective-permute-start | bytes 3538952 | tf_op jit(solution)/shard_map/ppermute | solution.py:12
  504.3 144.5 %collective-permute-start.23 = (bf16[1,384,1536]{1,2,0:T(8,128)(2,1)}, bf16[1,384,1536]{1,2,0:T(8,128)(2,1)S(1)}, u32[]{:S(2)}, u32[]{:S(2)}) collective-permute-start(bf16[1,384,1536]{1,2,0:T(8,128)(2,1)} %maximum_bitcast_fusion), channel_id=1, source_target_pairs={{19,0},{20,1},{21,2},{22,3},{23,4},{24,5},{25,6},{26,7},{27,8},{28... | collective-permute-start | bytes 3538952 | tf_op jit(solution)/shard_map/ppermute | solution.py:12
  549.5 99.6 %collective-permute-start.24 = (bf16[1,384,1536]{1,2,0:T(8,128)(2,1)}, bf16[1,384,1536]{1,2,0:T(8,128)(2,1)S(1)}, u32[]{:S(2)}, u32[]{:S(2)}) collective-permute-start(bf16[1,384,1536]{1,2,0:T(8,128)(2,1)} %maximum_bitcast_fusion), channel_id=1, source_target_pairs={{20,0},{21,1},{22,2},{23,3},{24,4},{25,5},{26,6},{27,7},{28,8},{29... | collective-permute-start | bytes 3538952 | tf_op jit(solution)/shard_map/ppermute | solution.py:12
  551.0 153.7 %collective-permute-start.25 = (bf16[1,384,1536]{1,2,0:T(8,128)(2,1)}, bf16[1,384,1536]{1,2,0:T(8,128)(2,1)S(1)}, u32[]{:S(2)}, u32[]{:S(2)}) collective-permute-start(bf16[1,384,1536]{1,2,0:T(8,128)(2,1)} %maximum_bitcast_fusion), channel_id=1, source_target_pairs={{21,0},{22,1},{23,2},{24,3},{25,4},{26,5},{27,6},{28,7},{29,8},{30... | collective-permute-start | bytes 3538952 | tf_op jit(solution)/shard_map/ppermute | solution.py:12
  704.9 10.8 %copy-start.2 = (bf16[6,384,128]{1,2,0:T(8,128)(2,1)S(1)}, bf16[6,384,128]{1,2,0:T(8,128)(2,1)}, u32[]{:S(2)}) copy-start(bf16[6,384,128]{1,2,0:T(8,128)(2,1)} %custom-call.1) | copy-start | bytes 1769476
  909.3 92.4 %copy-start.3 = (f32[3072]{0:T(1024)S(1)}, f32[3072]{0:T(1024)}, u32[]{:S(2)}) copy-start(f32[3072]{0:T(1024)} %param.18) | copy-start | bytes 36868
  909.3 94.9 %copy-start.1 = (f32[128]{0:T(128)S(1)}, f32[128]{0:T(128)}, u32[]{:S(2)}) copy-start(f32[128]{0:T(128)} %param.15) | copy-start | bytes 1540
Sparse Core Ops, SparseCore 0:
  13.5 43.2 all-gather.1
  915.3 86.3 reduce-scatter.1
where the time goes:
time: 1010 us
  waiting for transfers between devices  477 us (47%)
  starting transfers between devices  276 us (27%)
  matrix products  139 us (14%)
  other arithmetic  67.1 us (7%)
  local copies, waits for them, and re-layouts  26.2 us (3%)
  between operations  14 us (1%)
  loops' own time  11.9 us (1%)
    ppermute x26, waiting for transfers between devices, shifted(): lax.ppermute(value, axis, [(source, source + steps) for source in range(l...  347 us
    ppermute x26, starting transfers between devices, shifted(): lax.ppermute(value, axis, [(source, source + steps) for source in range(l...  276 us
    reduce_scatter x1, waiting for transfers between devices, on_device(): lax.psum_scatter(jnp.dot(attention, out_weight, preferred_element_type=jn...  86.5 us
    dot_general x6, matrix products, one_head(): jnp.einsum('qok,okd->qd', weights, value_rows, preferred_element_type=jnp...  62.2 us
    dot_general x6, matrix products, one_head(): jnp.einsum('qd,okd->qok', query_rows, key_rows, preferred_element_type=jn...  59.5 us
    reduce_sum x6, other arithmetic, soft_weights(): jnp.sum(raised, axis=(1, 2), keepdims=True)  55.5 us
    all_gather x1, waiting for transfers between devices, on_device(): lax.all_gather(normed, 'heads', axis=0, tiled=True)  43.4 us
  transfers between devices with their start and end apart: 28, of which 15 were waited for; matrix products, arithmetic and copies ran while one was open for 1% of the time, Pallas kernels for 0%

commit v1 on v0

--- a/solution.py
+++ b/solution.py
@@ -4,6 +4,11 @@
 from jax.sharding import PartitionSpec as P
 
 GT = 4
+
+
+def balance_tokens(sheet, group_axis):
+    v_now = lax.all_to_all(jnp.stack([sheet] * lax.psum(1, group_axis), axis=0), group_axis, 0, 0)
+    return jnp.concatenate(v_now, axis=0)
 
 
 def shifted(value, axis, steps):
@@ -83,9 +88,7 @@
     group_heads = group_width // head_dim
     normed = modulate(tokens[0], mod_shift, mod_scale)
     projected = jnp.dot(
-        lax.all_gather(normed, "heads", axis=0, tiled=True),
-        qkv_weight,
-        preferred_element_type=jnp.float32,
+        balance_tokens(normed, "heads"), qkv_weight, preferred_element_type=jnp.float32
     ).astype(jnp.bfloat16)
     tile_tok = projected.shape[0]
     pieces = projected.reshape(tile_tok, group_heads, 3, head_dim)

time: 1010 us -> 1020 us (level)
    reduce_scatter x1, waiting for transfers between devices: 86.5 us -> 134 us  [on_device(): lax.psum_scatter(jnp.dot(attention, out_weight, preferred_element_type=jn...]
    all_gather x1 -> x0, waiting for transfers between devices: 43.4 us -> none  [on_device(): lax.all_gather(normed, 'heads', axis=0, tiled=True)]
    ppermute x26, waiting for transfers between devices: 347 us -> 312 us  [shifted(): lax.ppermute(value, axis, [(source, source + steps) for source in range(l...]
    all_to_all x0 -> x1, waiting for transfers between devices: none -> 28.3 us  [balance_tokens(): lax.all_to_all(jnp.stack([sheet] * lax.psum(1, group_axis), axis=0), grou...]
where the time goes in v1:
time: 1020 us
  waiting for transfers between devices  474 us (46%)
  starting transfers between devices  286 us (28%)
  matrix products  138 us (14%)
  other arithmetic  67.2 us (7%)
  local copies, waits for them, and re-layouts  27.9 us (3%)
  between operations  14 us (1%)
  loops' own time  11.9 us (1%)
    ppermute x26, waiting for transfers between devices, shifted(): lax.ppermute(value, axis, [(source, source + steps) for source in range(l...  312 us
    ppermute x26, starting transfers between devices, shifted(): lax.ppermute(value, axis, [(source, source + steps) for source in range(l...  280 us
    reduce_scatter x1, waiting for transfers between devices, on_device(): lax.psum_scatter(jnp.dot(attention, out_weight, preferred_element_type=jn...  134 us
    dot_general x6, matrix products, one_head(): jnp.einsum('qok,okd->qd', weights, value_rows, preferred_element_type=jnp...  62.2 us
    dot_general x6, matrix products, one_head(): jnp.einsum('qd,okd->qok', query_rows, key_rows, preferred_element_type=jn...  59.5 us
    reduce_sum x6, other arithmetic, soft_weights(): jnp.sum(raised, axis=(1, 2), keepdims=True)  55.5 us
    all_to_all x1, waiting for transfers between devices, balance_tokens(): lax.all_to_all(jnp.stack([sheet] * lax.psum(1, group_axis), axis=0), grou...  28.3 us
  transfers between devices with their start and end apart: 28, of which 15 were waited for; matrix products, arithmetic and copies ran while one was open for 1% of the time, Pallas kernels for 0%

profile of v1, /device:TPU:1, one launch (start us, length us, event | category | flops | bytes accessed | tf_op | source)
XLA Modules:
  0.0 1018.5 jit_solution(16637109274758059174)
XLA Ops:
  7.3 1.5 convert_reduce_fusion
  8.9 1.7 fusion.28
  11.9 1.6 pad_maximum_fusion
  13.5 5.7 all-to-all-start
  19.2 28.3 %all-to-all-done = bf16[2,192,3072]{2,1,0:T(8,128)(2,1)S(1)} async-done(((bf16[2,192,3072]{2,1,0:T(8,128)(2,1)}), bf16[2,192,3072]{2,1,0:T(8,128)(2,1)S(1)}, u32[]{:S(2)}, u32[]{:S(2)}) %all-to-all-start) | async-done | bytes 2359328 | tf_op jit(solution)/shard_map/all_to_all | solution.py:10
  47.5 10.2 %convolution_convert_fusion.1 = bf16[384,2304]{1,0:T(8,128)(2,1)} fusion(bf16[384,3072]{1,0:T(8,128)(2,1)S(1)} %bitcast.99, bf16[3072,2304]{1,0:T(8,128)(2,1)} %param.12), kind=kOutput, calls=%fused_computation.21 | convolution fusion | flops 5436702720 | bytes 18284544 | tf_op jit(solution)/shard_map/dot_general | solution.py:90
  57.7 2.8 copy.14
  62.1 9.7 collective-permute-start
  71.9 2.7 collective-permute-start.1
  74.6 5.3 collective-permute-start.2
  80.0 1.4 collective-permute-start.3
  81.4 2.2 collective-permute-start.4
  83.9 7.3 collective-permute-done
  91.2 21.4 %collective-permute-start.5 = (bf16[1,384,1536]{1,2,0:T(8,128)(2,1)}, bf16[1,384,1536]{1,2,0:T(8,128)(2,1)S(1)}, u32[]{:S(2)}, u32[]{:S(2)}) collective-permute-start(bf16[1,384,1536]{1,2,0:T(8,128)(2,1)} %maximum_bitcast_fusion), channel_id=1, source_target_pairs={{0,15},{1,16},{2,17},{3,18},{4,19},{5,20},{6,21},{7,22},{8,23},{9,... | collective-permute-start | bytes 3538952 | tf_op jit(solution)/shard_map/ppermute | solution.py:17
  112.6 1.4 constant_dynamic-update-slice_fusion.27
  114.0 48.3 %collective-permute-start.6 = (bf16[1,384,1536]{1,2,0:T(8,128)(2,1)}, bf16[1,384,1536]{1,2,0:T(8,128)(2,1)S(1)}, u32[]{:S(2)}, u32[]{:S(2)}) collective-permute-start(bf16[1,384,1536]{1,2,0:T(8,128)(2,1)} %maximum_bitcast_fusion), channel_id=1, source_target_pairs={{0,13},{1,14},{2,15},{3,16},{4,17},{5,18},{6,19},{7,20},{8,21},{9,... | collective-permute-start | bytes 3538952 | tf_op jit(solution)/shard_map/ppermute | solution.py:17
  162.3 1.5 constant_dynamic-update-slice_fusion.26
  163.8 24.3 %collective-permute-start.7 = (bf16[1,384,1536]{1,2,0:T(8,128)(2,1)}, bf16[1,384,1536]{1,2,0:T(8,128)(2,1)S(1)}, u32[]{:S(2)}, u32[]{:S(2)}) collective-permute-start(bf16[1,384,1536]{1,2,0:T(8,128)(2,1)} %maximum_bitcast_fusion), channel_id=1, source_target_pairs={{0,12},{1,13},{2,14},{3,15},{4,16},{5,17},{6,18},{7,19},{8,20},{9,... | collective-permute-start | bytes 3538952 | tf_op jit(solution)/shard_map/ppermute | solution.py:17
  188.1 1.5 constant_dynamic-update-slice_fusion.25
  189.7 38.3 %collective-permute-start.8 = (bf16[1,384,1536]{1,2,0:T(8,128)(2,1)}, bf16[1,384,1536]{1,2,0:T(8,128)(2,1)S(1)}, u32[]{:S(2)}, u32[]{:S(2)}) collective-permute-start(bf16[1,384,1536]{1,2,0:T(8,128)(2,1)} %maximum_bitcast_fusion), channel_id=1, source_target_pairs={{0,11},{1,12},{2,13},{3,14},{4,15},{5,16},{6,17},{7,18},{8,19},{9,... | collective-permute-start | bytes 3538952 | tf_op jit(solution)/shard_map/ppermute | solution.py:17
  228.2 103.0 %collective-permute-start.9 = (bf16[1,384,1536]{1,2,0:T(8,128)(2,1)}, bf16[1,384,1536]{1,2,0:T(8,128)(2,1)S(1)}, u32[]{:S(2)}, u32[]{:S(2)}) collective-permute-start(bf16[1,384,1536]{1,2,0:T(8,128)(2,1)} %maximum_bitcast_fusion), channel_id=1, source_target_pairs={{0,5},{1,6},{2,7},{3,8},{4,9},{5,10},{6,11},{7,12},{8,13},{9,14},{... | collective-permute-start | bytes 3538952 | tf_op jit(solution)/shard_map/ppermute | solution.py:17
  331.5 1.4 collective-permute-start.10
  333.1 1.4 collective-permute-start.11
  334.7 3.3 collective-permute-start.12
  338.3 1.9 collective-permute-start.13
  340.5 31.9 %collective-permute-done.9 = bf16[1,384,1536]{1,2,0:T(8,128)(2,1)S(1)} collective-permute-done((bf16[1,384,1536]{1,2,0:T(8,128)(2,1)}, bf16[1,384,1536]{1,2,0:T(8,128)(2,1)S(1)}, u32[]{:S(2)}, u32[]{:S(2)}) %collective-permute-start.9) | collective-permute-done | bytes 1179680 | tf_op jit(solution)/shard_map/ppermute | solution.py:17
  373.9 1.3 collective-permute-start.15
  377.1 11.1 %collective-permute-done.12 = bf16[1,384,1536]{1,2,0:T(8,128)(2,1)S(1)} collective-permute-done((bf16[1,384,1536]{1,2,0:T(8,128)(2,1)}, bf16[1,384,1536]{1,2,0:T(8,128)(2,1)S(1)}, u32[]{:S(2)}, u32[]{:S(2)}) %collective-permute-start.12) | collective-permute-done | bytes 1179680 | tf_op jit(solution)/shard_map/ppermute | solution.py:17
  390.0 4.1 collective-permute-done.13
  394.0 1.3 collective-permute-start.18
  395.6 38.6 %collective-permute-done.14 = bf16[1,384,1536]{1,2,0:T(8,128)(2,1)S(1)} collective-permute-done((bf16[1,384,1536]{1,2,0:T(8,128)(2,1)}, bf16[1,384,1536]{1,2,0:T(8,128)(2,1)S(1)}, u32[]{:S(2)}, u32[]{:S(2)}) %collective-permute-start.14) | collective-permute-done | bytes 1179680 | tf_op jit(solution)/shard_map/ppermute | solution.py:17
  434.2 1.5 collective-permute-start.19
  435.9 1.3 collective-permute-start.20
  437.4 34.9 %collective-permute-done.16 = bf16[1,384,1536]{1,2,0:T(8,128)(2,1)S(1)} collective-permute-done((bf16[1,384,1536]{1,2,0:T(8,128)(2,1)}, bf16[1,384,1536]{1,2,0:T(8,128)(2,1)S(1)}, u32[]{:S(2)}, u32[]{:S(2)}) %collective-permute-start.16) | collective-permute-done | bytes 1179680 | tf_op jit(solution)/shard_map/ppermute | solution.py:17
  473.8 9.4 collective-permute-done.17
  484.8 11.4 %collective-permute-done.18 = bf16[1,384,1536]{1,2,0:T(8,128)(2,1)S(1)} collective-permute-done((bf16[1,384,1536]{1,2,0:T(8,128)(2,1)}, bf16[1,384,1536]{1,2,0:T(8,128)(2,1)S(1)}, u32[]{:S(2)}, u32[]{:S(2)}) %collective-permute-start.18) | collective-permute-done | bytes 1179680 | tf_op jit(solution)/shard_map/ppermute | solution.py:17
  497.7 44.3 %collective-permute-done.19 = bf16[1,384,1536]{1,2,0:T(8,128)(2,1)S(1)} collective-permute-done((bf16[1,384,1536]{1,2,0:T(8,128)(2,1)}, bf16[1,384,1536]{1,2,0:T(8,128)(2,1)S(1)}, u32[]{:S(2)}, u32[]{:S(2)}) %collective-permute-start.19) | collective-permute-done | bytes 1179680 | tf_op jit(solution)/shard_map/ppermute | solution.py:17
  543.6 1.3 collective-permute-start.25
  545.4 8.4 collective-permute-done.22
  554.0 71.5 %collective-permute-done.23 = bf16[1,384,1536]{1,2,0:T(8,128)(2,1)S(1)} collective-permute-done((bf16[1,384,1536]{1,2,0:T(8,128)(2,1)}, bf16[1,384,1536]{1,2,0:T(8,128)(2,1)S(1)}, u32[]{:S(2)}, u32[]{:S(2)}) %collective-permute-start.23) | collective-permute-done | bytes 1179680 | tf_op jit(solution)/shard_map/ppermute | solution.py:17
  626.0 39.2 %collective-permute-done.25 = bf16[1,384,1536]{1,2,0:T(8,128)(2,1)S(1)} collective-permute-done((bf16[1,384,1536]{1,2,0:T(8,128)(2,1)}, bf16[1,384,1536]{1,2,0:T(8,128)(2,1)S(1)}, u32[]{:S(2)}, u32[]{:S(2)}) %collective-permute-start.25) | collective-permute-done | bytes 1179680 | tf_op jit(solution)/shard_map/ppermute | solution.py:17
  665.4 10.8 %fusion.44 = (bf16[27,384,768]{1,2,0:T(8,128)(2,1)}, bf16[27,384,768]{1,2,0:T(8,128)(2,1)}) fusion(bf16[27,384,1536]{1,2,0:T(8,128)(2,1)S(1)} %constant_dynamic-update-slice_fusion.1), kind=kLoop, calls=%fused_computation.99 | loop fusion | bytes 63700992 | tf_op jit(solution)/shard_map/slice | solution.py:107
  676.2 193.5 %while.10 = (s32[]{:T(128)}, bf16[6,384,128]{1,2,0:T(8,128)(2,1)S(1)}, pred[27]{0:T(512)(128)(4,1)S(1)}, s32[6]{0:T(128)S(1)}, bf16[384,6,128]{0,2,1:T(8,128)(2,...) while((s32[]{:T(128)}, ...), condition=%wide.region_7.8_spmd, body=%wide.region_4.7_spmd.sunk | while | flops 2082274560 | bytes 53683416 | solution.py:120
  678.7 9.9 select_reduce_fusion.2
  688.7 9.3 fusion.53
  697.9 10.4 %fusion.54 = bf16[1,384,128]{2,1,0:T(8,128)(2,1)S(1)} fusion(bf16[27,384,6,128]{1,3,2,0:T(8,128)(2,1)} %get-tuple-element.143, s32[]{:T(128)S(6)} %select_n.126, f32[384,27,384]{0,2,1:T(8,128)} %get-tuple-element.115, f32[384]{0:T(512)S(1)} %fusion.53, f32[384]{0:T(512)S(1)} %get-tuple-element.116, pred[27]{0:T(512)(128)(4,1)S(1)} %get-tuple-element.139), kind=kOutput, calls=%fused_computation.12.clone.1 | convolution fusion | flops 1039171584 | bytes 18680864 | tf_op jit(solution)/shard_map/while/body/eval_jaxpr/qok,okd->qd/dot_general | solution.py:116
  711.0 9.9 select_reduce_fusion.2
  720.9 9.3 fusion.53
  730.2 10.4 %fusion.54 = bf16[1,384,128]{2,1,0:T(8,128)(2,1)S(1)} fusion(bf16[27,384,6,128]{1,3,2,0:T(8,128)(2,1)} %get-tuple-element.143, s32[]{:T(128)S(6)} %select_n.126, f32[384,27,384]{0,2,1:T(8,128)} %get-tuple-element.115, f32[384]{0:T(512)S(1)} %fusion.53, f32[384]{0:T(512)S(1)} %get-tuple-element.116, pred[27]{0:T(512)(128)(4,1)S(1)} %get-tuple-element.139), kind=kOutput, calls=%fused_computation.12.clone.1 | convolution fusion | flops 1039171584 | bytes 18680864 | tf_op jit(solution)/shard_map/while/body/eval_jaxpr/qok,okd->qd/dot_general | solution.py:116
  743.2 9.9 select_reduce_fusion.2
  753.2 9.3 fusion.53
  762.4 10.4 %fusion.54 = bf16[1,384,128]{2,1,0:T(8,128)(2,1)S(1)} fusion(bf16[27,384,6,128]{1,3,2,0:T(8,128)(2,1)} %get-tuple-element.143, s32[]{:T(128)S(6)} %select_n.126, f32[384,27,384]{0,2,1:T(8,128)} %get-tuple-element.115, f32[384]{0:T(512)S(1)} %fusion.53, f32[384]{0:T(512)S(1)} %get-tuple-element.116, pred[27]{0:T(512)(128)(4,1)S(1)} %get-tuple-element.139), kind=kOutput, calls=%fused_computation.12.clone.1 | convolution fusion | flops 1039171584 | bytes 18680864 | tf_op jit(solution)/shard_map/while/body/eval_jaxpr/qok,okd->qd/dot_general | solution.py:116
  775.5 9.9 select_reduce_fusion.2
  785.4 9.3 fusion.53
  794.7 10.4 %fusion.54 = bf16[1,384,128]{2,1,0:T(8,128)(2,1)S(1)} fusion(bf16[27,384,6,128]{1,3,2,0:T(8,128)(2,1)} %get-tuple-element.143, s32[]{:T(128)S(6)} %select_n.126, f32[384,27,384]{0,2,1:T(8,128)} %get-tuple-element.115, f32[384]{0:T(512)S(1)} %fusion.53, f32[384]{0:T(512)S(1)} %get-tuple-element.116, pred[27]{0:T(512)(128)(4,1)S(1)} %get-tuple-element.139), kind=kOutput, calls=%fused_computation.12.clone.1 | convolution fusion | flops 1039171584 | bytes 18680864 | tf_op jit(solution)/shard_map/while/body/eval_jaxpr/qok,okd->qd/dot_general | solution.py:116
  807.7 9.9 select_reduce_fusion.2
  817.7 9.3 fusion.53
  826.9 10.4 %fusion.54 = bf16[1,384,128]{2,1,0:T(8,128)(2,1)S(1)} fusion(bf16[27,384,6,128]{1,3,2,0:T(8,128)(2,1)} %get-tuple-element.143, s32[]{:T(128)S(6)} %select_n.126, f32[384,27,384]{0,2,1:T(8,128)} %get-tuple-element.115, f32[384]{0:T(512)S(1)} %fusion.53, f32[384]{0:T(512)S(1)} %get-tuple-element.116, pred[27]{0:T(512)(128)(4,1)S(1)} %get-tuple-element.139), kind=kOutput, calls=%fused_computation.12.clone.1 | convolution fusion | flops 1039171584 | bytes 18680864 | tf_op jit(solution)/shard_map/while/body/eval_jaxpr/qok,okd->qd/dot_general | solution.py:116
  840.0 9.9 select_reduce_fusion.2
  849.9 9.3 fusion.53
  859.2 10.4 %fusion.54 = bf16[1,384,128]{2,1,0:T(8,128)(2,1)S(1)} fusion(bf16[27,384,6,128]{1,3,2,0:T(8,128)(2,1)} %get-tuple-element.143, s32[]{:T(128)S(6)} %select_n.126, f32[384,27,384]{0,2,1:T(8,128)} %get-tuple-element.115, f32[384]{0:T(512)S(1)} %fusion.53, f32[384]{0:T(512)S(1)} %get-tuple-element.116, pred[27]{0:T(512)(128)(4,1)S(1)} %get-tuple-element.139), kind=kOutput, calls=%fused_computation.12.clone.1 | convolution fusion | flops 1039171584 | bytes 18680864 | tf_op jit(solution)/shard_map/while/body/eval_jaxpr/qok,okd->qd/dot_general | solution.py:116
  869.7 5.8 convolution_convert_fusion
  875.6 133.6 %reduce-scatter.2.cloned.1.call-done = bf16[192,3072]{1,0:T(8,128)(2,1)} async-done(((bf16[384,3072]{1,0:T(8,128)(2,1)}), bf16[192,3072]{1,0:T(8,128)(2,1)}) %reduce-scatter.2.cloned.1.call-update) | async-done | bytes 1179664 | tf_op jit(solution)/shard_map/reduce_scatter | solution.py:122
  1009.2 2.5 fusion.33
  (95 shorter events, 23.3 us)
Async XLA Ops:
  6.5 12.7 %copy-start = (f32[128]{0:T(128)S(1)}, f32[128]{0:T(128)}, u32[]{:S(2)}) copy-start(f32[128]{0:T(128)} %param.15) | copy-start | bytes 1540
  6.5 4.1 copy-start.2
  13.5 34.0 %all-to-all-start = ((bf16[2,192,3072]{2,1,0:T(8,128)(2,1)}), bf16[2,192,3072]{2,1,0:T(8,128)(2,1)S(1)}, u32[]{:S(2)}, u32[]{:S(2)}) async-start(bf16[2,192,3072]{2,1,0:T(8,128)(2,1)} %pad_maximum_fusion), calls=%async_computation | async-start | bytes 4718592 | tf_op jit(solution)/shard_map/all_to_all | solution.py:10
  19.2 990.0 %reduce-scatter.2.cloned.1.call-start = ((), (), s32[]{:S(2)}) async-start(), calls=%async_computation.2 | async-start | bytes 3538944 | tf_op jit(solution)/shard_map/reduce_scatter | solution.py:122
  60.6 19.3 %copy-start.6 = (s32[1,27]{1,0:T(1,128)S(1)}, s32[1,27]{1,0:T(1,128)}, u32[]{:S(2)}) copy-start(s32[1,27]{1,0:T(1,128)} %param.19) | copy-start | bytes 328
  60.6 23.1 %copy-start.5 = (f32[128]{0:T(128)S(1)}, f32[128]{0:T(128)}, u32[]{:S(2)}) copy-start(f32[128]{0:T(128)} %param.14) | copy-start | bytes 1540
  62.1 29.1 %collective-permute-start = (bf16[1,384,1536]{1,2,0:T(8,128)(2,1)}, bf16[1,384,1536]{1,2,0:T(8,128)(2,1)}, u32[]{:S(2)}, u32[]{:S(2)}) collective-permute-start(bf16[1,384,1536]{1,2,0:T(8,128)(2,1)} %maximum_bitcast_fusion), channel_id=1, source_target_pairs={{0,21},{1,22},{2,23},{3,24},{4,25},{5,26},{6,27},{7,28},{8,29},{9,... | collective-permute-start | bytes 3538952 | tf_op jit(solution)/shard_map/ppermute | solution.py:17
  71.9 42.1 %collective-permute-start.1 = (bf16[1,384,1536]{1,2,0:T(8,128)(2,1)}, bf16[1,384,1536]{1,2,0:T(8,128)(2,1)}, u32[]{:S(2)}, u32[]{:S(2)}) collective-permute-start(bf16[1,384,1536]{1,2,0:T(8,128)(2,1)} %maximum_bitcast_fusion), channel_id=1, source_target_pairs={{0,20},{1,21},{2,22},{3,23},{4,24},{5,25},{6,26},{7,27},{8,28},{9,... | collective-permute-start | bytes 3538952 | tf_op jit(solution)/shard_map/ppermute | solution.py:17
  74.6 89.2 %collective-permute-start.2 = (bf16[1,384,1536]{1,2,0:T(8,128)(2,1)}, bf16[1,384,1536]{1,2,0:T(8,128)(2,1)}, u32[]{:S(2)}, u32[]{:S(2)}) collective-permute-start(bf16[1,384,1536]{1,2,0:T(8,128)(2,1)} %maximum_bitcast_fusion), channel_id=1, source_target_pairs={{0,19},{1,20},{2,21},{3,22},{4,23},{5,24},{6,25},{7,26},{8,27},{9,... | collective-permute-start | bytes 3538952 | tf_op jit(solution)/shard_map/ppermute | solution.py:17
  80.0 109.7 %collective-permute-start.3 = (bf16[1,384,1536]{1,2,0:T(8,128)(2,1)}, bf16[1,384,1536]{1,2,0:T(8,128)(2,1)S(1)}, u32[]{:S(2)}, u32[]{:S(2)}) collective-permute-start(bf16[1,384,1536]{1,2,0:T(8,128)(2,1)} %maximum_bitcast_fusion), channel_id=1, source_target_pairs={{0,17},{1,18},{2,19},{3,20},{4,21},{5,22},{6,23},{7,24},{8,25},{9,... | collective-permute-start | bytes 3538952 | tf_op jit(solution)/shard_map/ppermute | solution.py:17
  81.4 146.9 %collective-permute-start.4 = (bf16[1,384,1536]{1,2,0:T(8,128)(2,1)}, bf16[1,384,1536]{1,2,0:T(8,128)(2,1)S(1)}, u32[]{:S(2)}, u32[]{:S(2)}) collective-permute-start(bf16[1,384,1536]{1,2,0:T(8,128)(2,1)} %maximum_bitcast_fusion), channel_id=1, source_target_pairs={{0,16},{1,17},{2,18},{3,19},{4,20},{5,21},{6,22},{7,23},{8,24},{9,... | collective-permute-start | bytes 3538952 | tf_op jit(solution)/shard_map/ppermute | solution.py:17
  91.2 240.2 %collective-permute-start.5 = (bf16[1,384,1536]{1,2,0:T(8,128)(2,1)}, bf16[1,384,1536]{1,2,0:T(8,128)(2,1)S(1)}, u32[]{:S(2)}, u32[]{:S(2)}) collective-permute-start(bf16[1,384,1536]{1,2,0:T(8,128)(2,1)} %maximum_bitcast_fusion), channel_id=1, source_target_pairs={{0,15},{1,16},{2,17},{3,18},{4,19},{5,20},{6,21},{7,22},{8,23},{9,... | collective-permute-start | bytes 3538952 | tf_op jit(solution)/shard_map/ppermute | solution.py:17
  114.0 219.1 %collective-permute-start.6 = (bf16[1,384,1536]{1,2,0:T(8,128)(2,1)}, bf16[1,384,1536]{1,2,0:T(8,128)(2,1)S(1)}, u32[]{:S(2)}, u32[]{:S(2)}) collective-permute-start(bf16[1,384,1536]{1,2,0:T(8,128)(2,1)} %maximum_bitcast_fusion), channel_id=1, source_target_pairs={{0,13},{1,14},{2,15},{3,16},{4,17},{5,18},{6,19},{7,20},{8,21},{9,... | collective-permute-start | bytes 3538952 | tf_op jit(solution)/shard_map/ppermute | solution.py:17
  163.8 170.9 %collective-permute-start.7 = (bf16[1,384,1536]{1,2,0:T(8,128)(2,1)}, bf16[1,384,1536]{1,2,0:T(8,128)(2,1)S(1)}, u32[]{:S(2)}, u32[]{:S(2)}) collective-permute-start(bf16[1,384,1536]{1,2,0:T(8,128)(2,1)} %maximum_bitcast_fusion), channel_id=1, source_target_pairs={{0,12},{1,13},{2,14},{3,15},{4,16},{5,17},{6,18},{7,19},{8,20},{9,... | collective-permute-start | bytes 3538952 | tf_op jit(solution)/shard_map/ppermute | solution.py:17
  189.7 148.6 %collective-permute-start.8 = (bf16[1,384,1536]{1,2,0:T(8,128)(2,1)}, bf16[1,384,1536]{1,2,0:T(8,128)(2,1)S(1)}, u32[]{:S(2)}, u32[]{:S(2)}) collective-permute-start(bf16[1,384,1536]{1,2,0:T(8,128)(2,1)} %maximum_bitcast_fusion), channel_id=1, source_target_pairs={{0,11},{1,12},{2,13},{3,14},{4,15},{5,16},{6,17},{7,18},{8,19},{9,... | collective-permute-start | bytes 3538952 | tf_op jit(solution)/shard_map/ppermute | solution.py:17
  228.2 144.1 %collective-permute-start.9 = (bf16[1,384,1536]{1,2,0:T(8,128)(2,1)}, bf16[1,384,1536]{1,2,0:T(8,128)(2,1)S(1)}, u32[]{:S(2)}, u32[]{:S(2)}) collective-permute-start(bf16[1,384,1536]{1,2,0:T(8,128)(2,1)} %maximum_bitcast_fusion), channel_id=1, source_target_pairs={{0,5},{1,6},{2,7},{3,8},{4,9},{5,10},{6,11},{7,12},{8,13},{9,14},{... | collective-permute-start | bytes 3538952 | tf_op jit(solution)/shard_map/ppermute | solution.py:17
  331.5 42.4 %collective-permute-start.10 = (bf16[1,384,1536]{1,2,0:T(8,128)(2,1)}, bf16[1,384,1536]{1,2,0:T(8,128)(2,1)S(1)}, u32[]{:S(2)}, u32[]{:S(2)}) collective-permute-start(bf16[1,384,1536]{1,2,0:T(8,128)(2,1)} %maximum_bitcast_fusion), channel_id=1, source_target_pairs={{0,4},{1,5},{2,6},{3,7},{4,8},{5,9},{6,10},{7,11},{8,12},{9,13},{1... | collective-permute-start | bytes 3538952 | tf_op jit(solution)/shard_map/ppermute | solution.py:17
  333.1 42.5 %collective-permute-start.11 = (bf16[1,384,1536]{1,2,0:T(8,128)(2,1)}, bf16[1,384,1536]{1,2,0:T(8,128)(2,1)S(1)}, u32[]{:S(2)}, u32[]{:S(2)}) collective-permute-start(bf16[1,384,1536]{1,2,0:T(8,128)(2,1)} %maximum_bitcast_fusion), channel_id=1, source_target_pairs={{0,3},{1,4},{2,5},{3,6},{4,7},{5,8},{6,9},{7,10},{8,11},{9,12},{10... | collective-permute-start | bytes 3538952 | tf_op jit(solution)/shard_map/ppermute | solution.py:17
  334.7 53.5 %collective-permute-start.12 = (bf16[1,384,1536]{1,2,0:T(8,128)(2,1)}, bf16[1,384,1536]{1,2,0:T(8,128)(2,1)S(1)}, u32[]{:S(2)}, u32[]{:S(2)}) collective-permute-start(bf16[1,384,1536]{1,2,0:T(8,128)(2,1)} %maximum_bitcast_fusion), channel_id=1, source_target_pairs={{0,1},{1,2},{2,3},{3,4},{4,5},{5,6},{6,7},{7,8},{8,9},{9,10},{10,1... | collective-permute-start | bytes 3538952 | tf_op jit(solution)/shard_map/ppermute | solution.py:17
  338.3 55.7 %collective-permute-start.13 = (bf16[1,384,1536]{1,2,0:T(8,128)(2,1)}, bf16[1,384,1536]{1,2,0:T(8,128)(2,1)S(1)}, u32[]{:S(2)}, u32[]{:S(2)}) collective-permute-start(bf16[1,384,1536]{1,2,0:T(8,128)(2,1)} %maximum_bitcast_fusion), channel_id=1, source_target_pairs={{1,0},{2,1},{3,2},{4,3},{5,4},{6,5},{7,6},{8,7},{9,8},{10,9},{11,1... | collective-permute-start | bytes 3538952 | tf_op jit(solution)/shard_map/ppermute | solution.py:17
  372.3 61.8 %collective-permute-start.14 = (bf16[1,384,1536]{1,2,0:T(8,128)(2,1)}, bf16[1,384,1536]{1,2,0:T(8,128)(2,1)S(1)}, u32[]{:S(2)}, u32[]{:S(2)}) collective-permute-start(bf16[1,384,1536]{1,2,0:T(8,128)(2,1)} %maximum_bitcast_fusion), channel_id=1, source_target_pairs={{3,0},{4,1},{5,2},{6,3},{7,4},{8,5},{9,6},{10,7},{11,8},{12,9},{13... | collective-permute-start | bytes 3538952 | tf_op jit(solution)/shard_map/ppermute | solution.py:17
  373.9 62.0 %collective-permute-start.15 = (bf16[1,384,1536]{1,2,0:T(8,128)(2,1)}, bf16[1,384,1536]{1,2,0:T(8,128)(2,1)S(1)}, u32[]{:S(2)}, u32[]{:S(2)}) collective-permute-start(bf16[1,384,1536]{1,2,0:T(8,128)(2,1)} %maximum_bitcast_fusion), channel_id=1, source_target_pairs={{4,0},{5,1},{6,2},{7,3},{8,4},{9,5},{10,6},{11,7},{12,8},{13,9},{1... | collective-permute-start | bytes 3538952 | tf_op jit(solution)/shard_map/ppermute | solution.py:17
  375.5 96.8 %collective-permute-start.16 = (bf16[1,384,1536]{1,2,0:T(8,128)(2,1)}, bf16[1,384,1536]{1,2,0:T(8,128)(2,1)S(1)}, u32[]{:S(2)}, u32[]{:S(2)}) collective-permute-start(bf16[1,384,1536]{1,2,0:T(8,128)(2,1)} %maximum_bitcast_fusion), channel_id=1, source_target_pairs={{5,0},{6,1},{7,2},{8,3},{9,4},{10,5},{11,6},{12,7},{13,8},{14,9},{... | collective-permute-start | bytes 3538952 | tf_op jit(solution)/shard_map/ppermute | solution.py:17
  388.2 95.1 %collective-permute-start.17 = (bf16[1,384,1536]{1,2,0:T(8,128)(2,1)}, bf16[1,384,1536]{1,2,0:T(8,128)(2,1)S(1)}, u32[]{:S(2)}, u32[]{:S(2)}) collective-permute-start(bf16[1,384,1536]{1,2,0:T(8,128)(2,1)} %maximum_bitcast_fusion), channel_id=1, source_target_pairs={{11,0},{12,1},{13,2},{14,3},{15,4},{16,5},{17,6},{18,7},{19,8},{20... | collective-permute-start | bytes 3538952 | tf_op jit(solution)/shard_map/ppermute | solution.py:17
  394.0 102.2 %collective-permute-start.18 = (bf16[1,384,1536]{1,2,0:T(8,128)(2,1)}, bf16[1,384,1536]{1,2,0:T(8,128)(2,1)S(1)}, u32[]{:S(2)}, u32[]{:S(2)}) collective-permute-start(bf16[1,384,1536]{1,2,0:T(8,128)(2,1)} %maximum_bitcast_fusion), channel_id=1, source_target_pairs={{12,0},{13,1},{14,2},{15,3},{16,4},{17,5},{18,6},{19,7},{20,8},{21... | collective-permute-start | bytes 3538952 | tf_op jit(solution)/shard_map/ppermute | solution.py:17
  434.2 107.9 %collective-permute-start.19 = (bf16[1,384,1536]{1,2,0:T(8,128)(2,1)}, bf16[1,384,1536]{1,2,0:T(8,128)(2,1)S(1)}, u32[]{:S(2)}, u32[]{:S(2)}) collective-permute-start(bf16[1,384,1536]{1,2,0:T(8,128)(2,1)} %maximum_bitcast_fusion), channel_id=1, source_target_pairs={{13,0},{14,1},{15,2},{16,3},{17,4},{18,5},{19,6},{20,7},{21,8},{22... | collective-permute-start | bytes 3538952 | tf_op jit(solution)/shard_map/ppermute | solution.py:17
  435.9 107.7 %collective-permute-start.20 = (bf16[1,384,1536]{1,2,0:T(8,128)(2,1)}, bf16[1,384,1536]{1,2,0:T(8,128)(2,1)S(1)}, u32[]{:S(2)}, u32[]{:S(2)}) collective-permute-start(bf16[1,384,1536]{1,2,0:T(8,128)(2,1)} %maximum_bitcast_fusion), channel_id=1, source_target_pairs={{15,0},{16,1},{17,2},{18,3},{19,4},{20,5},{21,6},{22,7},{23,8},{24... | collective-permute-start | bytes 3538952 | tf_op jit(solution)/shard_map/ppermute | solution.py:17
  472.3 72.8 %collective-permute-start.21 = (bf16[1,384,1536]{1,2,0:T(8,128)(2,1)}, bf16[1,384,1536]{1,2,0:T(8,128)(2,1)S(1)}, u32[]{:S(2)}, u32[]{:S(2)}) collective-permute-start(bf16[1,384,1536]{1,2,0:T(8,128)(2,1)} %maximum_bitcast_fusion), channel_id=1, source_target_pairs={{16,0},{17,1},{18,2},{19,3},{20,4},{21,5},{22,6},{23,7},{24,8},{25... | collective-permute-start | bytes 3538952 | tf_op jit(solution)/shard_map/ppermute | solution.py:17
  483.3 70.5 %collective-permute-start.22 = (bf16[1,384,1536]{1,2,0:T(8,128)(2,1)}, bf16[1,384,1536]{1,2,0:T(8,128)(2,1)S(1)}, u32[]{:S(2)}, u32[]{:S(2)}) collective-permute-start(bf16[1,384,1536]{1,2,0:T(8,128)(2,1)} %maximum_bitcast_fusion), channel_id=1, source_target_pairs={{17,0},{18,1},{19,2},{20,3},{21,4},{22,5},{23,6},{24,7},{25,8},{26... | collective-permute-start | bytes 3538952 | tf_op jit(solution)/shard_map/ppermute | solution.py:17
  496.2 129.3 %collective-permute-start.23 = (bf16[1,384,1536]{1,2,0:T(8,128)(2,1)}, bf16[1,384,1536]{1,2,0:T(8,128)(2,1)S(1)}, u32[]{:S(2)}, u32[]{:S(2)}) collective-permute-start(bf16[1,384,1536]{1,2,0:T(8,128)(2,1)} %maximum_bitcast_fusion), channel_id=1, source_target_pairs={{19,0},{20,1},{21,2},{22,3},{23,4},{24,5},{25,6},{26,7},{27,8},{28... | collective-permute-start | bytes 3538952 | tf_op jit(solution)/shard_map/ppermute | solution.py:17
  542.0 83.7 %collective-permute-start.24 = (bf16[1,384,1536]{1,2,0:T(8,128)(2,1)}, bf16[1,384,1536]{1,2,0:T(8,128)(2,1)S(1)}, u32[]{:S(2)}, u32[]{:S(2)}) collective-permute-start(bf16[1,384,1536]{1,2,0:T(8,128)(2,1)} %maximum_bitcast_fusion), channel_id=1, source_target_pairs={{20,0},{21,1},{22,2},{23,3},{24,4},{25,5},{26,6},{27,7},{28,8},{29... | collective-permute-start | bytes 3538952 | tf_op jit(solution)/shard_map/ppermute | solution.py:17
  543.6 121.5 %collective-permute-start.25 = (bf16[1,384,1536]{1,2,0:T(8,128)(2,1)}, bf16[1,384,1536]{1,2,0:T(8,128)(2,1)S(1)}, u32[]{:S(2)}, u32[]{:S(2)}) collective-permute-start(bf16[1,384,1536]{1,2,0:T(8,128)(2,1)} %maximum_bitcast_fusion), channel_id=1, source_target_pairs={{21,0},{22,1},{23,2},{24,3},{25,4},{26,5},{27,6},{28,7},{29,8},{30... | collective-permute-start | bytes 3538952 | tf_op jit(solution)/shard_map/ppermute | solution.py:17
  665.4 10.8 %copy-start.3 = (bf16[6,384,128]{1,2,0:T(8,128)(2,1)S(1)}, bf16[6,384,128]{1,2,0:T(8,128)(2,1)}, u32[]{:S(2)}) copy-start(bf16[6,384,128]{1,2,0:T(8,128)(2,1)} %custom-call.1) | copy-start | bytes 1769476
  869.7 139.5 %copy-start.4 = (f32[3072]{0:T(1024)S(1)}, f32[3072]{0:T(1024)}, u32[]{:S(2)}) copy-start(f32[3072]{0:T(1024)} %param.18) | copy-start | bytes 36868
  869.7 142.0 %copy-start.1 = (f32[128]{0:T(128)S(1)}, f32[128]{0:T(128)}, u32[]{:S(2)}) copy-start(f32[128]{0:T(128)} %param.15) | copy-start | bytes 1540
Sparse Core Ops, SparseCore 0:
  875.7 133.4 reduce-scatter.1
